TPU v7x, 256 devices: a whole 4x4x8 slice. The times are simulated.
256 devices in a mesh: dp: 16 (over x_hi, y, core), tensor: 16 (over z, x_lo).
Axes of the slice: x: 4 (x_hi: 2, x_lo: 2; x = x_hi * 2 + x_lo), y: 4, z: 8, core: 2. Of those that a mesh axis runs over, the one named last changes fastest.
Arguments:
- out_grad: bfloat16 [8192, 4096], P('dp', 'tensor'), may hold values from -6 to 6
- gate_act: bfloat16 [8192, 14336], P('dp', 'tensor'), may hold values from -8 to 8
- up_act: bfloat16 [8192, 14336], P('dp', 'tensor'), may hold values from -6 to 6
- w_down: bfloat16 [4096, 14336], P('dp', 'tensor'), may hold values from -0.09375 to 0.09375
Outputs:
- gate_grad: bfloat16 [8192, 14336], P('dp', 'tensor')
- up_grad: bfloat16 [8192, 14336], P('dp', 'tensor')
- down_grad: bfloat16 [4096, 14336], P('dp', 'tensor')
All inputs are finite; a program needn't handle non-finite values.
Results may differ from a plain program's by a relative error of at most 0.0049.
Values may be sent and summed in bfloat16 or wider, within the bound.
A program may use at most 128 MiB of HBM per device.

v0:
```python
import math
import jax
import jax.numpy as jnp
from jax import lax
from jax.sharding import PartitionSpec as P


def weight_total(rows_all, hidden):
    return lax.psum_scatter(
        lax.dot_general(
            rows_all, hidden, (((0,), (0,)), ((), ())), preferred_element_type=jnp.float32
        ),
        "dp",
        scatter_dimension=0,
        tiled=True,
    )


def body(out_grad, gate_act, up_act, w_down):
    seq_rows = gate_act.shape[0]
    grad_scale = 1.0 / math.sqrt(seq_rows * lax.axis_size("dp"))
    gate_wide = gate_act.astype(jnp.float32)
    up_wide = up_act.astype(jnp.float32)
    sigmoid_gate = jax.nn.sigmoid(gate_wide)
    activated = gate_wide * sigmoid_gate
    hidden = (activated * up_wide).astype(jnp.bfloat16)
    rows_all = lax.all_gather(out_grad, "tensor", axis=1, tiled=True)
    hidden_grad = jnp.dot(
        rows_all,
        lax.all_gather(w_down, "dp", axis=0, tiled=True),
        preferred_element_type=jnp.float32,
    )
    summed = weight_total(rows_all, hidden)
    gate_grad = (
        hidden_grad * up_wide * sigmoid_gate * (1.0 + gate_wide * (1.0 - sigmoid_gate))
    ).astype(jnp.bfloat16)
    up_grad = (hidden_grad * activated).astype(jnp.bfloat16)
    down_grad = (summed * grad_scale).astype(jnp.bfloat16)
    return (gate_grad, up_grad, down_grad)


def solution(mesh):
    placed = (P("dp", "tensor"), P("dp", "tensor"), P("dp", "tensor"), P("dp", "tensor"))
    return jax.shard_map(
        body,
        mesh=mesh,
        in_specs=placed,
        out_specs=(P("dp", "tensor"), P("dp", "tensor"), P("dp", "tensor")),
        check_vma=False,
    )
```

profile of v0, /device:TPU:1, one launch (start us, length us, event | category | flops | bytes accessed | tf_op | source)
XLA Modules:
  0.0 361.3 jit_solution(15101293496528034004)
XLA Ops:
  7.2 0.0 all-gather.3.cloned.1.call-start
  7.2 0.7 all-gather.3.cloned.1.call-update
  7.9 0.0 all-gather.5.cloned.1.call-start
  7.9 0.7 all-gather.5.cloned.1.call-update
  8.6 0.0 reduce-scatter.2.cloned.1.call-start
  8.7 116.5 %all-gather.3.cloned.1.call-done = bf16[512,4096]{1,0:T(8,128)(2,1)} async-done(((bf16[512,256]{1,0:T(8,128)(2,1)}), bf16[512,4096]{1,0:T(8,128)(2,1)}) %all-gather.3.cloned.1.call-update) | async-done | bytes 4194320 | tf_op jit(solution)/shard_map/all_gather | solution.py:27
  125.2 12.1 %convolution_bitcast_fusion = f32[4096,896]{0,1:T(8,128)} fusion(bf16[512,4096]{1,0:T(8,128)(2,1)} %all-gather.3.cloned.1.call-done, bf16[512,896]{1,0:T(8,128)(2,1)} %param.6, bf16[512,896]{1,0:T(8,128)(2,1)} %param.5), kind=kOutput, calls=%fused_computation | convolution fusion | flops 3761766400 | bytes 20709376 | tf_op jit(solution)/shard_map/dot_general | solution.py:10
  137.2 0.0 copy-start
  137.2 0.0 copy-start.1
  137.3 0.0 reduce-scatter.2.cloned.1.call-update
  137.3 73.7 %all-gather.5.cloned.1.call-done = bf16[4096,896]{1,0:T(8,128)(2,1)} async-done(((bf16[256,896]{1,0:T(8,128)(2,1)}), bf16[4096,896]{1,0:T(8,128)(2,1)}) %all-gather.5.cloned.1.call-update) | async-done | bytes 7340048 | tf_op jit(solution)/shard_map/all_gather | solution.py:30
  211.0 0.0 copy-done
  211.0 0.0 copy-done.1
  211.0 10.5 %multiply_convert_fusion = (bf16[512,896]{1,0:T(8,128)(2,1)}, bf16[512,896]{1,0:T(8,128)(2,1)}) fusion(bf16[512,896]{1,0:T(8,128)(2,1)S(1)} %copy-done, bf16[512,896]{1,0:T(8,128)(2,1)S(1)} %copy-done.1, bf16[512,4096]{1,0:T(8,128)(2,1)} %all-gather.3.cloned.1.call-done, bf16[4096,896]{1,0:T(8,128)(2,1)} %all-gather.5.cloned.1.call-done), kind=kOutput, calls=%fused_computation.14 | convolution fusion | flops 3764977664 | bytes 15204352 | tf_op jit(solution)/shard_map/dot_general | solution.py:28
  221.5 131.0 %reduce-scatter.2.cloned.1.call-done = f32[256,896]{0,1:T(8,128)} async-done(((f32[4096,896]{0,1:T(8,128)}), f32[256,896]{0,1:T(8,128)}) %reduce-scatter.2.cloned.1.call-update) | async-done | bytes 917520 | tf_op jit(solution)/shard_map/reduce_scatter | solution.py:9
  352.6 1.3 multiply_convert_fusion.1
  353.8 1.0 copy.7
Async XLA Ops:
  7.2 118.0 %all-gather.3.cloned.1.call-start = ((), (), s32[]{:S(2)}) async-start(), calls=%async_computation.1 | async-start | bytes 4456448 | tf_op jit(solution)/shard_map/all_gather | solution.py:27
  7.9 203.1 %all-gather.5.cloned.1.call-start = ((), (), s32[]{:S(2)}) async-start(), calls=%async_computation.2 | async-start | bytes 7798784 | tf_op jit(solution)/shard_map/all_gather | solution.py:30
  8.6 343.9 %reduce-scatter.2.cloned.1.call-start = ((), (), s32[]{:S(2)}) async-start(), calls=%async_computation.3 | async-start | bytes 15597568 | tf_op jit(solution)/shard_map/reduce_scatter | solution.py:9
  137.2 73.8 %copy-start = (bf16[512,896]{1,0:T(8,128)(2,1)S(1)}, bf16[512,896]{1,0:T(8,128)(2,1)}, u32[]{:S(2)}) copy-start(bf16[512,896]{1,0:T(8,128)(2,1)} %param.5) | copy-start | bytes 2752516
  137.2 73.8 %copy-start.1 = (bf16[512,896]{1,0:T(8,128)(2,1)S(1)}, bf16[512,896]{1,0:T(8,128)(2,1)}, u32[]{:S(2)}) copy-start(bf16[512,896]{1,0:T(8,128)(2,1)} %param.6) | copy-start | bytes 2752516
Sparse Core Ops, SparseCore 0:
  9.7 115.4 all-gather.2
  127.9 83.0 all-gather.4
  215.6 136.9 reduce-scatter.1
where the time goes:
time: 361 us
  waiting for transfers between devices  323 us (89%)
  matrix products  22.6 us (6%)
  between operations  13.7 us (4%)
    reduce_scatter x1, waiting for transfers between devices, weight_total(): lax.psum_scatter(lax.dot_general(rows_all, hidden, (((0,), (0,)), ((), ()...  131 us
    all_gather x1, waiting for transfers between devices, body(): rows_all = lax.all_gather(out_grad, 'tensor', axis=1, tiled=True)  116 us
    all_gather x1, waiting for transfers between devices, body(): lax.all_gather(w_down, 'dp', axis=0, tiled=True)  73.7 us
    dot_general x1, matrix products, weight_total(): lax.dot_general(rows_all, hidden, (((0,), (0,)), ((), ())), preferred_ele...  12.1 us
    dot_general x1, matrix products, body(): jnp.dot(rows_all, lax.all_gather(w_down, 'dp', axis=0, tiled=True), prefe...  10.5 us
  transfers between devices with their start and end apart: 3, of which 3 were waited for; matrix products, arithmetic and copies ran while one was open for 6% of the time, Pallas kernels for 0%

commit v1 on v0

--- a/solution.py
+++ b/solution.py
@@ -27,7 +27,9 @@
     rows_all = lax.all_gather(out_grad, "tensor", axis=1, tiled=True)
     hidden_grad = jnp.dot(
         rows_all,
-        lax.all_gather(w_down, "dp", axis=0, tiled=True),
+        jnp.concatenate(
+            lax.all_to_all(jnp.stack([w_down] * lax.axis_size("dp")), "dp", 0, 0), axis=0
+        ),
         preferred_element_type=jnp.float32,
     )
     summed = weight_total(rows_all, hidden)

time: 361 us -> 331 us (0.917)
  waiting for transfers between devices: 323 us -> 176 us
  blocking collectives: 0 us -> 117 us
  matrix products: 22.6 us -> 18.3 us
    all_to_all x0 -> x1, blocking collectives: none -> 117 us  [body(): lax.all_to_all(jnp.stack([w_down] * lax.axis_size('dp')), 'dp', 0, 0)]
    all_gather x1 -> x0, waiting for transfers between devices: 73.7 us -> none  [body(): lax.all_gather(w_down, 'dp', axis=0, tiled=True)]
    reduce_scatter x1, waiting for transfers between devices: 131 us -> 58.6 us  [weight_total(): lax.psum_scatter(lax.dot_general(rows_all, hidden, (((0,), (0,)), ((), ()...]
    dot_general x1, matrix products: 10.5 us -> 6.22 us  [body(): jnp.dot(rows_all, jnp.concatenate(lax.all_to_all(jnp.stack([w_down] * lax...]
  transfers between devices with their start and end apart: 3 -> 2, of which waited for: 3 -> 2; matrix products, arithmetic and copies ran while one was open for 6% -> 2% of each run, Pallas kernels for 0% -> 0%
where the time goes in v1:
time: 331 us; the launch traced here: 330 us
  waiting for transfers between devices  176 us (53%)
  blocking collectives  117 us (35%)
  matrix products  18.3 us (6%)
  between operations  14.1 us (4%)
    all_to_all x1, blocking collectives, body(): lax.all_to_all(jnp.stack([w_down] * lax.axis_size('dp')), 'dp', 0, 0)  117 us
    all_gather x1, waiting for transfers between devices, body(): rows_all = lax.all_gather(out_grad, 'tensor', axis=1, tiled=True)  117 us
    reduce_scatter x1, waiting for transfers between devices, weight_total(): lax.psum_scatter(lax.dot_general(rows_all, hidden, (((0,), (0,)), ((), ()...  58.6 us
    dot_general x1, matrix products, weight_total(): lax.dot_general(rows_all, hidden, (((0,), (0,)), ((), ())), preferred_ele...  12.1 us
  transfers between devices with their start and end apart: 2, of which 2 were waited for; matrix products, arithmetic and copies ran while one was open for 2% of the time, Pallas kernels for 0%

profile of v1, /device:TPU:1, one launch (start us, length us, event | category | flops | bytes accessed | tf_op | source)
XLA Modules:
  0.0 330.4 jit_solution(6349233815737780528)
XLA Ops:
  7.2 0.0 all-gather.2.cloned.1.call-start
  7.2 0.7 all-gather.2.cloned.1.call-update
  7.9 0.0 reduce-scatter.2.cloned.1.call-start
  7.9 117.2 %all-gather.2.cloned.1.call-done = bf16[512,4096]{1,0:T(8,128)(2,1)} async-done(((bf16[512,256]{1,0:T(8,128)(2,1)}), bf16[512,4096]{1,0:T(8,128)(2,1)}) %all-gather.2.cloned.1.call-update) | async-done | bytes 4194320 | tf_op jit(solution)/shard_map/all_gather | solution.py:27
  125.2 12.1 %convolution_bitcast_fusion = f32[4096,896]{0,1:T(8,128)} fusion(bf16[512,4096]{1,0:T(8,128)(2,1)} %all-gather.2.cloned.1.call-done, bf16[512,896]{1,0:T(8,128)(2,1)} %param.6, bf16[512,896]{1,0:T(8,128)(2,1)} %param.5), kind=kOutput, calls=%fused_computation | convolution fusion | flops 3761766400 | bytes 20709376 | tf_op jit(solution)/shard_map/dot_general | solution.py:10
  137.2 0.0 copy-start.3
  137.2 0.0 reduce-scatter.2.cloned.1.call-update
  137.3 1.0 copy-done.3
  138.3 1.0 stack.2
  139.3 0.0 copy-start
  139.3 0.0 copy-start.1
  139.3 0.0 copy-start.2
  139.3 117.3 %all_to_all.5 = bf16[16,256,896]{2,1,0:T(8,128)(2,1)S(1)} all-to-all(bf16[16,256,896]{2,1,0:T(8,128)(2,1)S(1)} %stack.2), channel_id=1, replica_groups=mesh['dp'=16,'tensor'=16] {'dp'}, dimensions={0} | all-to-all | bytes 14680064 | tf_op jit(solution)/shard_map/all_to_all | solution.py:31
  256.6 0.0 copy-done
  256.6 0.0 copy-done.1
  256.6 0.0 copy-done.2
  256.6 6.2 %multiply_convert_fusion = (bf16[512,896]{1,0:T(8,128)(2,1)}, bf16[512,896]{1,0:T(8,128)(2,1)}) fusion(bf16[512,896]{1,0:T(8,128)(2,1)S(1)} %copy-done.1, bf16[512,896]{1,0:T(8,128)(2,1)S(1)} %copy-done.2, bf16[512,4096]{1,0:T(8,128)(2,1)S(1)} %copy-done, bf16[4096,896]{1,0:T(8,128)(2,1)S(1)} %bitcast.6), kind=kOutput, calls=%fused_computation.14 | convolution fusion | flops 3764977664 | bytes 15204352 | tf_op jit(solution)/shard_map/dot_general | solution.py:28
  262.8 58.6 %reduce-scatter.2.cloned.1.call-done = f32[256,896]{0,1:T(8,128)} async-done(((f32[4096,896]{0,1:T(8,128)}), f32[256,896]{0,1:T(8,128)}) %reduce-scatter.2.cloned.1.call-update) | async-done | bytes 917520 | tf_op jit(solution)/shard_map/reduce_scatter | solution.py:9
  321.4 1.3 multiply_convert_fusion.1
  322.6 1.0 copy.7
Async XLA Ops:
  7.2 118.0 %all-gather.2.cloned.1.call-start = ((), (), s32[]{:S(2)}) async-start(), calls=%async_computation.2 | async-start | bytes 4456448 | tf_op jit(solution)/shard_map/all_gather | solution.py:27
  7.9 313.5 %reduce-scatter.2.cloned.1.call-start = ((), (), s32[]{:S(2)}) async-start(), calls=%async_computation.3 | async-start | bytes 15597568 | tf_op jit(solution)/shard_map/reduce_scatter | solution.py:9
  137.2 1.0 copy-start.3
  139.3 117.3 %copy-start = (bf16[512,4096]{1,0:T(8,128)(2,1)S(1)}, bf16[512,4096]{1,0:T(8,128)(2,1)}, u32[]{:S(2)}) copy-start(bf16[512,4096]{1,0:T(8,128)(2,1)} %all-gather.2.cloned.1.call-done) | copy-start | bytes 12582916
  139.3 117.3 %copy-start.1 = (bf16[512,896]{1,0:T(8,128)(2,1)S(1)}, bf16[512,896]{1,0:T(8,128)(2,1)}, u32[]{:S(2)}) copy-start(bf16[512,896]{1,0:T(8,128)(2,1)} %param.5) | copy-start | bytes 2752516
  139.3 117.3 %copy-start.2 = (bf16[512,896]{1,0:T(8,128)(2,1)S(1)}, bf16[512,896]{1,0:T(8,128)(2,1)}, u32[]{:S(2)}) copy-start(bf16[512,896]{1,0:T(8,128)(2,1)} %param.6) | copy-start | bytes 2752516
Sparse Core Ops, SparseCore 0:
  9.7 115.4 all-gather.1
  137.4 183.9 reduce-scatter.1
